TPU v7x, 512 devices: a whole 4x8x8 slice. The times are simulated.
512 devices in a mesh: expert: 32 (over y, x), tensor: 16 (over z, core).
Axes of the slice: x: 4, y: 8, z: 8, core: 2. Of those that a mesh axis runs over, the one named last changes fastest.
Arguments:
- residual: bfloat16 [2048, 7168], P('expert', 'tensor'), may hold values from -40 to 40
- attn_parts: bfloat16 [16, 2048, 7168], P('tensor', 'expert'), may hold values from -2 to 2
- norm_gain: bfloat16 [7168], P('tensor'), may hold values from 0.099609375 to 1.8984375
- routes: int32 [2048, 8], P('expert'), may hold values from 0 to 31, all different within a row; in each aligned block of 64 rows (0 to 63, 64 to 127, ...) at most 24 rows name the same one
- route_weights: float32 [2048, 8], P('expert'), may hold values from 0.05 to 0.6
- w_gate: bfloat16 [32, 7168, 2048], P('expert', None, 'tensor'), may hold values from -0.06023809 to 0.06023809
- w_gate_q: bfloat16 [32, 7168, 2048], P('expert', None, 'tensor'), may hold values from -0.09567226 to 0.09567226
Outputs:
- token_error: float32 [2048], P('expert')
- expert_error: float32 [32], P('expert')
- hess_diag: float32 [32, 7168], P('expert', 'tensor')
Inputs may be any that keep to these rules, and one draw needn't show every extreme that they name: `routes`: no expert is named by more than 24 of the rows of one device, and in every draw some expert is named by exactly 24 of them; the 8 experts of a token are distinct; every expert is named by some token.
All inputs are finite; a program needn't handle non-finite values.
Results may differ from a plain program's by a relative error of at most 0.0023.
Values may be sent and summed in bfloat16 or wider, within the bound.
A program may use at most 64 MiB of HBM per device.

v0:
```python
import jax
import jax.numpy as jnp
from jax import lax
from jax.sharding import PartitionSpec as P

D = 7168
FF = 2048
CAP = 24
epsilon = 1e-06


def per_device(residual, attn_parts, norm_gain, routes, route_weights, w_gate, w_gate_q):
    n_expert = lax.axis_size("expert")
    tok_count = residual.shape[0]
    local_cols = residual.shape[1]
    top_count = routes.shape[1]
    gain_wide = norm_gain.astype(jnp.float32)[None, :]
    summed = lax.psum_scatter(
        attn_parts[0].astype(jnp.float32).astype(jnp.bfloat16),
        "tensor",
        scatter_dimension=1,
        tiled=True,
    ).astype(jnp.float32)
    hidden = residual.astype(jnp.float32) + summed
    squares = lax.psum(jnp.sum(hidden * hidden, axis=1), "tensor")
    scaling = lax.rsqrt(squares / D + epsilon)
    normed = (hidden * scaling[:, None] * gain_wide).astype(jnp.bfloat16)
    expert_ids = jnp.arange(n_expert, dtype=jnp.int32)
    flat_routes = routes.reshape(-1)
    one_hot = (flat_routes[:, None] == expert_ids[None, :]).astype(jnp.int32)
    earlier = jnp.cumsum(one_hot, axis=0) - one_hot
    slot_index = jnp.sum(earlier * one_hot, axis=1)
    target = flat_routes * CAP + slot_index
    load_counts = jnp.sum(one_hot, axis=0)
    slot_ids = jnp.arange(n_expert * CAP, dtype=jnp.int32)
    placing = (slot_ids[:, None] == target[None, :]).reshape(n_expert * CAP, tok_count, top_count)
    dispatch = jnp.sum(placing.astype(jnp.int32), axis=2).astype(jnp.bfloat16)
    count_send = load_counts.astype(jnp.bfloat16).reshape(n_expert, 1)
    weight_full = w_gate[0]
    weight_quant = w_gate_q[0]
    outgoing = jnp.dot(dispatch, normed, preferred_element_type=jnp.float32).astype(jnp.bfloat16)
    outgoing = outgoing.reshape(n_expert, CAP, local_cols)
    arrived, arrived_counts = (
        lax.all_to_all(outgoing, "expert", split_axis=0, concat_axis=0, tiled=True),
        lax.all_to_all(count_send, "expert", split_axis=0, concat_axis=0, tiled=True),
    )
    own_block = arrived.reshape(n_expert * CAP, local_cols)
    column_block = lax.all_gather(own_block, "tensor", axis=1, tiled=True)
    full_acc = jnp.dot(column_block, weight_full, preferred_element_type=jnp.float32)
    quant_acc = jnp.dot(column_block, weight_quant, preferred_element_type=jnp.float32)
    block_squares = jnp.einsum("rc,rc->c", own_block, own_block, preferred_element_type=jnp.float32)
    total_load = jnp.sum(arrived_counts.astype(jnp.float32))
    hess_local = 2.0 * block_squares / total_load
    difference = full_acc - quant_acc
    err_part = (jnp.sum(difference * difference, axis=1) / FF).reshape(n_expert, CAP)
    pow_part = (jnp.sum(full_acc * full_acc, axis=1) / FF).reshape(n_expert, CAP)
    err_slots, pow_slots = lax.psum((err_part, pow_part), "tensor")
    expert_total = jnp.sum(err_slots) / (jnp.sum(pow_slots) + epsilon)
    back_err, back_pow = (
        lax.all_to_all(err_slots, "expert", split_axis=0, concat_axis=0, tiled=True),
        lax.all_to_all(pow_slots, "expert", split_axis=0, concat_axis=0, tiled=True),
    )
    token_err = jnp.take(back_err.reshape(-1), target).reshape(tok_count, top_count)
    token_pow = jnp.take(back_pow.reshape(-1), target).reshape(tok_count, top_count)
    ratios = token_err / (token_pow + epsilon)
    token_error = jnp.sum(route_weights * ratios, axis=1)
    return (token_error, expert_total.reshape(1), hess_local.reshape(1, local_cols))


def solution(mesh):
    placed = (
        P("expert", "tensor"),
        P("tensor", "expert", None),
        P("tensor"),
        P("expert", None),
        P("expert", None),
        P("expert", None, "tensor"),
        P("expert", None, "tensor"),
    )
    return jax.shard_map(
        per_device,
        mesh=mesh,
        in_specs=placed,
        out_specs=(P("expert"), P("expert"), P("expert", "tensor")),
        check_vma=False,
    )
```

profile of v0, /device:TPU:2, one launch (start us, length us, event | category | flops | bytes accessed | tf_op | source)
XLA Modules:
  0.0 304.8 jit_solution(2115498877063809150)
XLA Ops:
  7.2 0.0 copy-start
  7.2 0.0 reduce-scatter.4.cloned.1.call-start
  7.2 0.0 copy-start.2
  7.2 0.0 copy-start.4
  7.2 2.7 copy.57
  10.0 0.0 copy-start.1
  10.0 0.0 reduce-scatter.4.cloned.1.call-update
  10.0 0.0 all-gather.2.cloned.1.call-start
  10.1 0.0 copy-done.2
  10.1 0.1 copy.40
  10.2 0.1 eq.40
  10.3 0.1 eq.44
  10.3 0.0 copy-done.4
  10.4 1.2 reduce-window.6
  11.6 0.2 slice_reduce_fusion
  11.8 0.2 convert_reduce_fusion.1
  12.0 0.1 reduce_sum.93
  12.1 0.1 copy.43
  12.1 0.1 copy.44
  12.2 0.5 convert_reduce_fusion
  12.8 65.0 %reduce-scatter.4.cloned.1.call-done = bf16[448,64]{1,0:T(8,128)(2,1)} async-done(((bf16[7168,64]{1,0:T(8,128)(2,1)}), bf16[448,64]{1,0:T(8,128)(2,1)}) %reduce-scatter.4.cloned.1.call-update) | async-done | bytes 57360
  77.8 1.0 copy.58
  78.8 0.0 copy-done.1
  78.8 0.1 multiply_reduce_fusion.1
  78.9 23.6 %psum.21 = f32[64]{0:T(128)S(1)} all-reduce(f32[64]{0:T(128)S(1)} %multiply_reduce_fusion.1), channel_id=1, replica_groups=mesh['expert'=32,'tensor'=16] {'tensor'}, use_global_device_ids=true, to_apply=%region_6.7 | all-reduce | flops 64 | bytes 512 | tf_op jit(solution)/shard_map/psum | solution.py:25
  102.6 0.5 convolution_convert_fusion
  103.0 0.3 copy.45
  103.3 0.0 copy-start.3
  103.3 32.0 %all_to_all.29 = bf16[32,24,448]{2,1,0:T(8,128)(2,1)S(1)} all-to-all(bf16[32,24,448]{2,1,0:T(8,128)(2,1)S(1)} %bitcast.49), channel_id=1, replica_groups=mesh['expert'=32,'tensor'=16] {'expert'}, dimensions={0} | all-to-all | bytes 1376256 | tf_op jit(solution)/shard_map/all_to_all | solution.py:44
  135.4 1.1 copy.46
  136.5 0.0 all-gather.2.cloned.1.call-update
  136.5 0.7 copy.50
  137.2 5.6 %all-to-all-start.3 = ((bf16[32,1,1]{2,1,0:T(2,128)(2,1)}), bf16[32,1,1]{2,1,0:T(2,128)(2,1)S(1)}, u32[]{:S(2)}, u32[]{:S(2)}) async-start(bf16[32,1,1]{2,1,0:T(2,128)(2,1)} %copy.50), calls=%async_computation.3 | async-start | bytes 32768 | tf_op jit(solution)/shard_map/all_to_all | solution.py:45
  142.8 0.0 copy-done.3
  142.8 0.1 copy.49
  142.9 8.4 %all-to-all-done.3 = bf16[32,1,1]{2,1,0:T(2,128)(2,1)S(1)} async-done(((bf16[32,1,1]{2,1,0:T(2,128)(2,1)}), bf16[32,1,1]{2,1,0:T(2,128)(2,1)S(1)}, u32[]{:S(2)}, u32[]{:S(2)}) %all-to-all-start.3) | async-done | bytes 96 | tf_op jit(solution)/shard_map/all_to_all | solution.py:45
  151.3 0.6 convert_reduce_fusion.2
  152.0 49.7 %all-gather.2.cloned.1.call-done = bf16[768,7168]{0,1:T(8,128)(2,1)} async-done(((bf16[768,448]{0,1:T(8,128)(2,1)}), bf16[768,7168]{0,1:T(8,128)(2,1)}) %all-gather.2.cloned.1.call-update) | async-done | bytes 11010064 | tf_op jit(solution)/shard_map/all_gather | solution.py:48
  201.7 0.0 copy-done
  201.7 0.0 copy-start.5
  201.7 6.0 %multiply_reduce_fusion = (f32[768]{0:T(1024)S(1)}, f32[768,128]{0,1:T(8,128)S(1)}) fusion(bf16[768,7168]{0,1:T(8,128)(2,1)} %all-gather.2.cloned.1.call-done, bf16[1,7168,128]{2,1,0:T(8,128)(2,1)S(1)} %copy-done), kind=kOutput, calls=%fused_computation.14 | convolution fusion | flops 1409481984 | bytes 13241344 | tf_op jit(solution)/shard_map/dot_general | solution.py:49
  207.7 1.2 copy-done.5
  208.9 0.5 copy-done.6
  209.4 1.8 fusion.11
  211.3 0.1 div.34
  211.3 0.1 div.36
  211.4 47.3 %all-reduce = (f32[32,24]{1,0:T(8,128)}, f32[32,24]{1,0:T(8,128)}) all-reduce(f32[32,24]{1,0:T(8,128)S(1)} %div.36, f32[32,24]{1,0:T(8,128)S(1)} %div.34), channel_id=1, replica_groups=mesh['expert'=32,'tensor'=16] {'tensor'}, use_global_device_ids=true, to_apply=%region_10.12 | all-reduce | flops 1536 | bytes 12288 | tf_op jit(solution)/shard_map/psum | solution.py:57
  258.7 9.9 %all-to-all-start.1 = ((f32[32,1,24]{2,1,0:T(1,128)}), f32[32,1,24]{2,1,0:T(1,128)S(1)}, u32[]{:S(2)}, u32[]{:S(2)}) async-start(f32[32,1,24]{2,1,0:T(1,128)} %bitcast.9), calls=%async_computation.1 | async-start | bytes 32768 | tf_op jit(solution)/shard_map/all_to_all | solution.py:60
  268.6 0.3 fusion.4
  268.9 8.3 %all-to-all-done.1 = f32[32,1,24]{2,1,0:T(1,128)S(1)} async-done(((f32[32,1,24]{2,1,0:T(1,128)}), f32[32,1,24]{2,1,0:T(1,128)S(1)}, u32[]{:S(2)}, u32[]{:S(2)}) %all-to-all-start.1) | async-done | bytes 3104 | tf_op jit(solution)/shard_map/all_to_all | solution.py:60
  277.1 5.0 %all-to-all-start.2 = ((f32[32,1,24]{2,1,0:T(1,128)}), f32[32,1,24]{2,1,0:T(1,128)S(1)}, u32[]{:S(2)}, u32[]{:S(2)}) async-start(f32[32,1,24]{2,1,0:T(1,128)} %bitcast.11), calls=%async_computation.2 | async-start | bytes 32768 | tf_op jit(solution)/shard_map/all_to_all | solution.py:61
  282.1 1.2 multiply_divide_fusion
  283.3 1.3 reduce_sum.99
  284.7 1.3 reduce_sum.100
  287.3 0.5 broadcast.60
  287.8 0.7 reduce.12
  288.5 0.1 reshape.113
  288.6 2.1 all-to-all-done.2
  290.7 0.7 reduce.11
  291.4 0.1 reshape.114
  291.5 2.3 gather_fusion
  293.8 2.3 gather_fusion.1
  296.1 0.1 div.38
  296.2 0.6 multiply_reduce_fusion.2
  (13 shorter events, 0.1 us)
Async XLA Ops:
  7.2 194.5 %copy-start = (bf16[1,7168,128]{2,1,0:T(8,128)(2,1)S(1)}, bf16[1,7168,128]{2,1,0:T(8,128)(2,1)}, u32[]{:S(2)}) copy-start(bf16[1,7168,128]{2,1,0:T(8,128)(2,1)} %param.14) | copy-start | bytes 5505028
  7.2 70.6 %reduce-scatter.4.cloned.1.call-start = ((), (), s32[]{:S(2)}) async-start(), calls=%async_computation.6 | async-start | bytes 1949696
  7.2 2.8 copy-start.2
  7.2 3.1 %copy-start.4 = (bf16[448]{0:T(512)(128)(2,1)S(1)}, bf16[448]{0:T(512)(128)(2,1)}, u32[]{:S(2)}) copy-start(bf16[448]{0:T(512)(128)(2,1)} %param.11) | copy-start | bytes 2692
  10.0 68.8 %copy-start.1 = (bf16[64,448]{1,0:T(8,128)(2,1)S(1)}, bf16[64,448]{1,0:T(8,128)(2,1)}, u32[]{:S(2)}) copy-start(bf16[64,448]{1,0:T(8,128)(2,1)} %param.9) | copy-start | bytes 172036
  10.0 191.6 %all-gather.2.cloned.1.call-start = ((), (), s32[]{:S(2)}) async-start(), calls=%async_computation.5 | async-start | bytes 11698176 | tf_op jit(solution)/shard_map/all_gather | solution.py:48
  103.3 39.5 %copy-start.3 = (f32[64,8]{0,1:T(8,128)S(1)}, f32[64,8]{0,1:T(8,128)}, u32[]{:S(2)}) copy-start(f32[64,8]{0,1:T(8,128)} %param.13) | copy-start | bytes 6148
  137.2 14.1 %all-to-all-start.3 = ((bf16[32,1,1]{2,1,0:T(2,128)(2,1)}), bf16[32,1,1]{2,1,0:T(2,128)(2,1)S(1)}, u32[]{:S(2)}, u32[]{:S(2)}) async-start(bf16[32,1,1]{2,1,0:T(2,128)(2,1)} %copy.50), calls=%async_computation.3 | async-start | bytes 32768 | tf_op jit(solution)/shard_map/all_to_all | solution.py:45
  201.7 7.3 %copy-start.5 = (bf16[768,7168]{0,1:T(8,128)(2,1)S(1)}, bf16[768,7168]{0,1:T(8,128)(2,1)}, u32[]{:S(2)}) copy-start(bf16[768,7168]{0,1:T(8,128)(2,1)} %all-gather.2.cloned.1.call-done) | copy-start | bytes 33030148
  201.7 7.8 %copy-start.6 = (bf16[1,7168,128]{2,1,0:T(8,128)(2,1)S(1)}, bf16[1,7168,128]{2,1,0:T(8,128)(2,1)}, u32[]{:S(2)}) copy-start(bf16[1,7168,128]{2,1,0:T(8,128)(2,1)} %param.15) | copy-start | bytes 5505028
  258.7 18.4 %all-to-all-start.1 = ((f32[32,1,24]{2,1,0:T(1,128)}), f32[32,1,24]{2,1,0:T(1,128)S(1)}, u32[]{:S(2)}, u32[]{:S(2)}) async-start(f32[32,1,24]{2,1,0:T(1,128)} %bitcast.9), calls=%async_computation.1 | async-start | bytes 32768 | tf_op jit(solution)/shard_map/all_to_all | solution.py:60
  277.1 13.6 %all-to-all-start.2 = ((f32[32,1,24]{2,1,0:T(1,128)}), f32[32,1,24]{2,1,0:T(1,128)S(1)}, u32[]{:S(2)}, u32[]{:S(2)}) async-start(f32[32,1,24]{2,1,0:T(1,128)} %bitcast.11), calls=%async_computation.2 | async-start | bytes 32768 | tf_op jit(solution)/shard_map/all_to_all | solution.py:61
Sparse Core Ops, SparseCore 0:
  10.9 66.9 reduce-scatter.3
  136.6 64.9 all-gather.1
where the time goes:
time: 305 us
  waiting for transfers between devices  134 us (44%)
  blocking collectives  103 us (34%)
  starting transfers between devices  20.5 us (7%)
  between operations  16.7 us (5%)
  local copies, waits for them, and re-layouts  13.9 us (5%)
  other arithmetic  8.86 us (3%)
  matrix products  8.29 us (3%)
    unnamed x3, waiting for transfers between devices  65.1 us
    all_gather x1, waiting for transfers between devices, per_device(): column_block = lax.all_gather(own_block, 'tensor', axis=1, tiled=True)  49.7 us
    psum x1, blocking collectives, per_device(): err_slots, pow_slots = lax.psum((err_part, pow_part), 'tensor')  47.3 us
    all_to_all x1, blocking collectives, per_device(): lax.all_to_all(outgoing, 'expert', split_axis=0, concat_axis=0, tiled=True)  32 us
    psum x1, blocking collectives, per_device(): squares = lax.psum(jnp.sum(hidden * hidden, axis=1), 'tensor')  23.6 us
    all_to_all x1, starting transfers between devices, per_device(): lax.all_to_all(err_slots, 'expert', split_axis=0, concat_axis=0, tiled=True)  9.87 us
    all_to_all x1, waiting for transfers between devices, per_device(): lax.all_to_all(count_send, 'expert', split_axis=0, concat_axis=0, tiled=T...  8.4 us
    all_to_all x1, waiting for transfers between devices, per_device(): lax.all_to_all(err_slots, 'expert', split_axis=0, concat_axis=0, tiled=True)  8.25 us
  transfers between devices with their start and end apart: 5, of which 5 were waited for; matrix products, arithmetic and copies ran while one was open for 3% of the time, Pallas kernels for 0%

commit v1 on v0

--- a/solution.py
+++ b/solution.py
@@ -45,7 +45,9 @@
         lax.all_to_all(count_send, "expert", split_axis=0, concat_axis=0, tiled=True),
     )
     own_block = arrived.reshape(n_expert * CAP, local_cols)
-    column_block = lax.all_gather(own_block, "tensor", axis=1, tiled=True)
+    column_block = jnp.concatenate(
+        lax.all_to_all(jnp.stack(lax.psum(1, "tensor") * [own_block], 0), "tensor", 0, 0), 1
+    )
     full_acc = jnp.dot(column_block, weight_full, preferred_element_type=jnp.float32)
     quant_acc = jnp.dot(column_block, weight_quant, preferred_element_type=jnp.float32)
     block_squares = jnp.einsum("rc,rc->c", own_block, own_block, preferred_element_type=jnp.float32)

time: 305 us -> 502 us (1.65)
  waiting for transfers between devices: 134 us -> 345 us
  blocking collectives: 103 us -> 70.6 us
  starting transfers between devices: 20.5 us -> 30.1 us
    all_to_all x0 -> x2, waiting for transfers between devices: none -> 261 us  [the longest x1 240 us: per_device(): lax.all_to_all(jnp.stack(lax.psum(1, 'tensor') * [own_block], 0), 'tensor...]
    all_gather x1 -> x0, waiting for transfers between devices: 49.7 us -> none  [per_device(): column_block = lax.all_gather(own_block, 'tensor', axis=1, tiled=True)]
    all_to_all x1 -> x0, blocking collectives: 32 us -> none  [per_device(): lax.all_to_all(outgoing, 'expert', split_axis=0, concat_axis=0, tiled=True)]
    all_to_all x0 -> x2, starting transfers between devices: none -> 14.9 us  [the longest x1 9.88 us: per_device(): lax.all_to_all(outgoing, 'expert', split_axis=0, concat_axis=0, tiled=True)]
    another operation x1 -> x3, local copies, waits for them, and re-layouts: 0.01 us -> 5.36 us  [the longest x2 5.36 us: per_device(): jnp.stack(lax.psum(1, 'tensor') * [own_block], 0)]
    all_to_all x1, starting transfers between devices: 9.87 us -> 4.71 us  [per_device(): lax.all_to_all(err_slots, 'expert', split_axis=0, concat_axis=0, tiled=True)]
    unnamed x3 -> x2, waiting for transfers between devices: 65.1 us -> 65.1 us
  transfers between devices with their start and end apart: 5 -> 6, of which waited for: 5 -> 6; matrix products, arithmetic and copies ran while one was open for 3% -> 2% of each run, Pallas kernels for 0% -> 0%
where the time goes in v1:
time: 502 us; the launch traced here: 501 us
  waiting for transfers between devices  345 us (69%)
  blocking collectives  70.6 us (14%)
  starting transfers between devices  30.1 us (6%)
  local copies, waits for them, and re-layouts  17.3 us (3%)
  between operations  16.7 us (3%)
  matrix products  12.4 us (2%)
  other arithmetic  8.87 us (2%)
    all_to_all x1, waiting for transfers between devices, per_device(): lax.all_to_all(jnp.stack(lax.psum(1, 'tensor') * [own_block], 0), 'tensor...  240 us
    unnamed x2, waiting for transfers between devices  65.1 us
    psum x1, blocking collectives, per_device(): err_slots, pow_slots = lax.psum((err_part, pow_part), 'tensor')  46.9 us
    psum x1, blocking collectives, per_device(): squares = lax.psum(jnp.sum(hidden * hidden, axis=1), 'tensor')  23.6 us
    all_to_all x1, waiting for transfers between devices, per_device(): lax.all_to_all(outgoing, 'expert', split_axis=0, concat_axis=0, tiled=True)  21.7 us
  transfers between devices with their start and end apart: 6, of which 6 were waited for; matrix products, arithmetic and copies ran while one was open for 2% of the time, Pallas kernels for 0%

profile of v1, /device:TPU:2, one launch (start us, length us, event | category | flops | bytes accessed | tf_op | source)
XLA Modules:
  0.0 501.1 jit_solution(15632526722423548934)
XLA Ops:
  7.2 0.0 copy-start
  7.2 0.0 reduce-scatter.4.cloned.1.call-start
  7.2 0.0 copy-start.2
  7.2 0.0 copy-start.4
  7.2 2.7 copy.59
  10.0 0.0 copy-start.1
  10.0 0.0 reduce-scatter.4.cloned.1.call-update
  10.0 0.0 copy-done.2
  10.0 0.1 copy.42
  10.1 0.1 eq.40
  10.2 0.1 eq.44
  10.3 0.0 copy-done.4
  10.3 1.2 reduce-window.6
  11.5 0.2 slice_reduce_fusion
  11.8 0.2 convert_reduce_fusion.1
  11.9 0.1 reduce_sum.93
  12.0 0.1 copy.45
  12.1 0.1 copy.46
  12.2 0.5 convert_reduce_fusion
  12.7 65.0 %reduce-scatter.4.cloned.1.call-done = bf16[448,64]{1,0:T(8,128)(2,1)} async-done(((bf16[7168,64]{1,0:T(8,128)(2,1)}), bf16[448,64]{1,0:T(8,128)(2,1)}) %reduce-scatter.4.cloned.1.call-update) | async-done | bytes 57360
  77.8 1.0 copy.60
  78.7 0.0 copy-done.1
  78.8 0.1 multiply_reduce_fusion.1
  78.9 23.6 %psum.21 = f32[64]{0:T(128)S(1)} all-reduce(f32[64]{0:T(128)S(1)} %multiply_reduce_fusion.1), channel_id=1, replica_groups=mesh['expert'=32,'tensor'=16] {'tensor'}, use_global_device_ids=true, to_apply=%region_6.7 | all-reduce | flops 64 | bytes 512 | tf_op jit(solution)/shard_map/psum | solution.py:25
  102.5 0.5 convolution_convert_fusion
  103.0 1.2 copy.47
  104.2 9.9 %all-to-all-start = ((bf16[32,24,448]{2,1,0:T(8,128)(2,1)}), bf16[32,24,448]{2,1,0:T(8,128)(2,1)S(1)}, u32[]{:S(2)}, u32[]{:S(2)}) async-start(bf16[32,24,448]{2,1,0:T(8,128)(2,1)} %bitcast.4), calls=%async_computation | async-start | bytes 1572864 | tf_op jit(solution)/shard_map/all_to_all | solution.py:44
  114.1 0.7 copy.52
  114.8 21.7 %all-to-all-done = bf16[32,24,448]{2,1,0:T(8,128)(2,1)S(1)} async-done(((bf16[32,24,448]{2,1,0:T(8,128)(2,1)}), bf16[32,24,448]{2,1,0:T(8,128)(2,1)S(1)}, u32[]{:S(2)}, u32[]{:S(2)}) %all-to-all-start) | async-done | bytes 688160 | tf_op jit(solution)/shard_map/all_to_all | solution.py:44
  136.4 5.6 %all-to-all-start.4 = ((bf16[32,1,1]{2,1,0:T(2,128)(2,1)}), bf16[32,1,1]{2,1,0:T(2,128)(2,1)S(1)}, u32[]{:S(2)}, u32[]{:S(2)}) async-start(bf16[32,1,1]{2,1,0:T(2,128)(2,1)} %copy.52), calls=%async_computation.4 | async-start | bytes 32768 | tf_op jit(solution)/shard_map/all_to_all | solution.py:45
  142.0 0.3 copy.48
  142.3 8.3 %all-to-all-done.4 = bf16[32,1,1]{2,1,0:T(2,128)(2,1)S(1)} async-done(((bf16[32,1,1]{2,1,0:T(2,128)(2,1)}), bf16[32,1,1]{2,1,0:T(2,128)(2,1)S(1)}, u32[]{:S(2)}, u32[]{:S(2)}) %all-to-all-start.4) | async-done | bytes 96 | tf_op jit(solution)/shard_map/all_to_all | solution.py:45
  150.5 5.1 %stack.3 = bf16[16,768,448]{1,2,0:T(8,128)(2,1)} broadcast(bf16[768,448]{0,1:T(8,128)(2,1)S(1)} %copy.48), dimensions={1,2} | broadcast | bytes 11698176 | tf_op jit(solution)/shard_map/stack | solution.py:49
  155.6 0.0 copy-start.3
  155.6 5.0 all-to-all-start.1
  160.6 0.0 copy-done.3
  160.6 0.1 copy.51
  160.7 0.6 convert_reduce_fusion.2
  161.4 239.6 %all-to-all-done.1 = bf16[16,768,448]{1,2,0:T(8,128)(2,1)} async-done(((bf16[16,768,448]{1,2,0:T(8,128)(2,1)}), bf16[16,768,448]{1,2,0:T(8,128)(2,1)}, u32[]{:S(2)}, u32[]{:S(2)}) %all-to-all-start.1) | async-done | bytes 11010080 | tf_op jit(solution)/shard_map/all_to_all | solution.py:49
  401.0 0.0 copy-done
  401.0 0.0 copy-start.5
  401.0 6.0 %multiply_reduce_fusion = (f32[768]{0:T(1024)S(1)}, f32[768,128]{0,1:T(8,128)S(1)}) fusion(bf16[768,7168]{0,1:T(8,128)(2,1)} %bitcast.7, bf16[1,7168,128]{2,1,0:T(8,128)(2,1)S(1)} %copy-done), kind=kOutput, calls=%fused_computation.14 | convolution fusion | flops 1409481984 | bytes 13241344 | tf_op jit(solution)/shard_map/dot_general | solution.py:51
  407.0 0.0 copy-done.5
  407.0 5.9 %fusion.11 = f32[768]{0:T(1024)S(1)} fusion(f32[768,128]{0,1:T(8,128)S(1)} %get-tuple-element.9, bf16[768,7168]{0,1:T(8,128)(2,1)} %bitcast.7, bf16[1,7168,128]{2,1,0:T(8,128)(2,1)S(1)} %copy-done.5), kind=kOutput, calls=%fused_computation.13 | convolution fusion | flops 1409580288 | bytes 13241344 | tf_op jit(solution)/shard_map/dot_general | solution.py:52
  413.0 0.1 div.34
  413.1 0.1 div.36
  413.1 46.9 %all-reduce = (f32[32,24]{1,0:T(8,128)}, f32[32,24]{1,0:T(8,128)}) all-reduce(f32[32,24]{1,0:T(8,128)S(1)} %div.36, f32[32,24]{1,0:T(8,128)S(1)} %div.34), channel_id=1, replica_groups=mesh['expert'=32,'tensor'=16] {'tensor'}, use_global_device_ids=true, to_apply=%region_10.12 | all-reduce | flops 1536 | bytes 12288 | tf_op jit(solution)/shard_map/psum | solution.py:59
  460.1 4.7 all-to-all-start.2
  464.8 0.3 fusion.4
  465.1 8.4 %all-to-all-done.2 = f32[32,1,24]{2,1,0:T(1,128)S(1)} async-done(((f32[32,1,24]{2,1,0:T(1,128)}), f32[32,1,24]{2,1,0:T(1,128)S(1)}, u32[]{:S(2)}, u32[]{:S(2)}) %all-to-all-start.2) | async-done | bytes 3104 | tf_op jit(solution)/shard_map/all_to_all | solution.py:62
  473.4 5.0 all-to-all-start.3
  478.4 1.2 multiply_divide_fusion
  479.6 1.3 reduce_sum.99
  481.0 1.3 reduce_sum.100
  483.6 0.5 broadcast.61
  484.1 0.7 reduce.12
  484.8 0.1 reshape.120
  484.9 2.1 all-to-all-done.3
  487.0 0.7 reduce.11
  487.7 0.1 reshape.121
  487.8 2.3 gather_fusion
  490.1 2.3 gather_fusion.1
  492.4 0.1 div.38
  492.5 0.6 multiply_reduce_fusion.2
  (12 shorter events, 0.1 us)
Async XLA Ops:
  7.2 393.8 %copy-start = (bf16[1,7168,128]{2,1,0:T(8,128)(2,1)S(1)}, bf16[1,7168,128]{2,1,0:T(8,128)(2,1)}, u32[]{:S(2)}) copy-start(bf16[1,7168,128]{2,1,0:T(8,128)(2,1)} %param.14) | copy-start | bytes 5505028
  7.2 70.6 %reduce-scatter.4.cloned.1.call-start = ((), (), s32[]{:S(2)}) async-start(), calls=%async_computation.6 | async-start | bytes 1949696
  7.2 2.8 copy-start.2
  7.2 3.1 copy-start.4
  10.0 68.8 %copy-start.1 = (bf16[64,448]{1,0:T(8,128)(2,1)S(1)}, bf16[64,448]{1,0:T(8,128)(2,1)}, u32[]{:S(2)}) copy-start(bf16[64,448]{1,0:T(8,128)(2,1)} %param.9) | copy-start | bytes 172036
  104.2 32.3 %all-to-all-start = ((bf16[32,24,448]{2,1,0:T(8,128)(2,1)}), bf16[32,24,448]{2,1,0:T(8,128)(2,1)S(1)}, u32[]{:S(2)}, u32[]{:S(2)}) async-start(bf16[32,24,448]{2,1,0:T(8,128)(2,1)} %bitcast.4), calls=%async_computation | async-start | bytes 1572864 | tf_op jit(solution)/shard_map/all_to_all | solution.py:44
  136.4 14.1 %all-to-all-start.4 = ((bf16[32,1,1]{2,1,0:T(2,128)(2,1)}), bf16[32,1,1]{2,1,0:T(2,128)(2,1)S(1)}, u32[]{:S(2)}, u32[]{:S(2)}) async-start(bf16[32,1,1]{2,1,0:T(2,128)(2,1)} %copy.52), calls=%async_computation.4 | async-start | bytes 32768 | tf_op jit(solution)/shard_map/all_to_all | solution.py:45
  155.6 5.0 copy-start.3
  155.6 245.4 %all-to-all-start.1 = ((bf16[16,768,448]{1,2,0:T(8,128)(2,1)}), bf16[16,768,448]{1,2,0:T(8,128)(2,1)}, u32[]{:S(2)}, u32[]{:S(2)}) async-start(bf16[16,768,448]{1,2,0:T(8,128)(2,1)} %stack.3), calls=%async_computation.1 | async-start | bytes 22020096 | tf_op jit(solution)/shard_map/all_to_all | solution.py:49
  401.0 6.0 %copy-start.5 = (bf16[1,7168,128]{2,1,0:T(8,128)(2,1)S(1)}, bf16[1,7168,128]{2,1,0:T(8,128)(2,1)}, u32[]{:S(2)}) copy-start(bf16[1,7168,128]{2,1,0:T(8,128)(2,1)} %param.15) | copy-start | bytes 5505028
  460.1 13.4 %all-to-all-start.2 = ((f32[32,1,24]{2,1,0:T(1,128)}), f32[32,1,24]{2,1,0:T(1,128)S(1)}, u32[]{:S(2)}, u32[]{:S(2)}) async-start(f32[32,1,24]{2,1,0:T(1,128)} %bitcast.12), calls=%async_computation.2 | async-start | bytes 32768 | tf_op jit(solution)/shard_map/all_to_all | solution.py:62
  473.4 13.6 %all-to-all-start.3 = ((f32[32,1,24]{2,1,0:T(1,128)}), f32[32,1,24]{2,1,0:T(1,128)S(1)}, u32[]{:S(2)}, u32[]{:S(2)}) async-start(f32[32,1,24]{2,1,0:T(1,128)} %bitcast.14), calls=%async_computation.3 | async-start | bytes 32768 | tf_op jit(solution)/shard_map/all_to_all | solution.py:63
Sparse Core Ops, SparseCore 0:
  10.9 66.8 reduce-scatter.3
